TPU v7x, 32 devices: a whole 2x2x4 slice. The times are simulated.
32 devices in a mesh: dp: 4 (over z), ctx: 8 (over y, x, core).
Axes of the slice: x: 2, y: 2, z: 4, core: 2. Of those that a mesh axis runs over, the one named last changes fastest.
Arguments:
- patches: bfloat16 [8, 1024, 6144], P('dp', 'ctx'), may hold values from -6 to 6
- w_in: bfloat16 [6144, 768], P(('dp', 'ctx')), may hold values from -0.078125 to 0.078125
- b_in: bfloat16 [768], P(('dp', 'ctx')), may hold values from -3 to 3
- g_one: bfloat16 [768], P(('dp', 'ctx')), may hold values from 0.25 to 1.75
- s_one: bfloat16 [768], P(('dp', 'ctx')), may hold values from -3 to 3
- w_qkv: bfloat16 [768, 2304], P(('dp', 'ctx')), may hold values from -0.21875 to 0.21875
- w_out: bfloat16 [768, 768], P(('dp', 'ctx')), may hold values from -1.75 to 1.75
- b_out: bfloat16 [768], P(('dp', 'ctx')), may hold values from -3 to 3
- g_two: bfloat16 [768], P(('dp', 'ctx')), may hold values from 0.25 to 1.75
- s_two: bfloat16 [768], P(('dp', 'ctx')), may hold values from -3 to 3
- w_up: bfloat16 [768, 3072], P(('dp', 'ctx')), may hold values from -0.21875 to 0.21875
- b_up: bfloat16 [3072], P(('dp', 'ctx')), may hold values from -3 to 3
- w_down: bfloat16 [3072, 768], P(('dp', 'ctx')), may hold values from -0.109375 to 0.109375
- b_down: bfloat16 [768], P(('dp', 'ctx')), may hold values from -3 to 3
- cotangent: bfloat16 [8, 1024, 768], P('dp', 'ctx'), may hold values from -6 to 6
Outputs:
- block_out: bfloat16 [8, 1024, 768], P('dp', 'ctx')
- grad_patches: float32 [8, 1024, 6144], P('dp', 'ctx')
- grad_w_in: float32 [6144, 768], P(('dp', 'ctx'))
- grad_b_in: float32 [768], P(('dp', 'ctx'))
- grad_g_one: float32 [768], P(('dp', 'ctx'))
- grad_s_one: float32 [768], P(('dp', 'ctx'))
- grad_w_qkv: float32 [768, 2304], P(('dp', 'ctx'))
- grad_w_out: float32 [768, 768], P(('dp', 'ctx'))
- grad_b_out: float32 [768], P(('dp', 'ctx'))
- grad_g_two: float32 [768], P(('dp', 'ctx'))
- grad_s_two: float32 [768], P(('dp', 'ctx'))
- grad_w_up: float32 [768, 3072], P(('dp', 'ctx'))
- grad_b_up: float32 [3072], P(('dp', 'ctx'))
- grad_w_down: float32 [3072, 768], P(('dp', 'ctx'))
- grad_b_down: float32 [768], P(('dp', 'ctx'))
All inputs are finite; a program needn't handle non-finite values.
Results may differ from a plain program's by a relative error of at most 0.015.
Values may be sent and summed in bfloat16 or wider, within the bound.
No kernel may reach another device: no remote copies, remote signals or barrier semaphores. Data moves between devices by JAX's collectives and lax.ppermute only.
A program may use at most 256 MiB of HBM per device.

v0:
```python
import jax
import jax.numpy as jnp
from jax import lax
from jax.sharding import PartitionSpec as P

HEADS = 12
HEAD = 64
eps_norm = 1e-05
gelu_coef = 0.7978845608028654


def norm_forward(stream, gain, shift):
    row_mean = jnp.mean(stream, axis=-1, keepdims=True)
    centered = stream - row_mean
    variance = jnp.mean(centered * centered, axis=-1, keepdims=True)
    inverse = lax.rsqrt(variance + eps_norm)
    normed = centered * inverse
    return (normed * gain + shift, normed, inverse)


def norm_backward(upstream, normed, inverse, gain):
    scaled = upstream * gain
    row_inner = jnp.mean(scaled, axis=-1, keepdims=True)
    row_corr = jnp.mean(scaled * normed, axis=-1, keepdims=True)
    stream_grad = inverse * (scaled - row_inner - normed * row_corr)
    return (stream_grad, jnp.sum(upstream * normed, axis=0), jnp.sum(upstream, axis=0))


def gelu_pair(pre_act):
    tanh_val = jnp.tanh(gelu_coef * (pre_act + 0.044715 * pre_act * pre_act * pre_act))
    gelu_out = 0.5 * pre_act * (1.0 + tanh_val)
    gelu_slope = 0.5 * (1.0 + tanh_val) + 0.5 * pre_act * (
        1.0 - tanh_val * tanh_val
    ) * gelu_coef * (1.0 + 3.0 * 0.044715 * pre_act * pre_act)
    return (gelu_out, gelu_slope)


def block_scores(queries, kv_all, key_block, key_width, offset):
    model_width = queries.shape[1] * queries.shape[2]
    kv_piece = lax.dynamic_slice_in_dim(kv_all, key_block * key_width, key_width, 0)
    key_rows = kv_piece[:, :model_width].reshape(key_width, HEADS, HEAD)
    value_rows = kv_piece[:, model_width:].reshape(key_width, HEADS, HEAD)
    scores = (
        jnp.einsum("qhd,khd->hqk", queries, key_rows, preferred_element_type=jnp.float32) * 0.125
    )
    key_pos = key_block * key_width + lax.iota(jnp.int32, key_width)
    row_pos = offset + lax.iota(jnp.int32, queries.shape[0])
    allowed = key_pos[None, :] <= row_pos[:, None]
    return (jnp.where(allowed[None], scores, -1e30), key_rows, value_rows)


def log_totals(queries, kv_all, key_width, offset, last_block):
    row_shape = (HEADS, queries.shape[0])

    def lse_step(key_block, state_pair):
        row_top, row_total = state_pair
        scores, key_rows, value_rows = block_scores(queries, kv_all, key_block, key_width, offset)
        new_top = jnp.maximum(row_top, jnp.max(scores, axis=-1))
        row_total = row_total * jnp.exp(row_top - new_top) + jnp.sum(
            jnp.exp(scores - new_top[..., None]), axis=-1
        )
        return (new_top, row_total)

    start_pair = (jnp.full(row_shape, -1e30, jnp.float32), jnp.zeros(row_shape, jnp.float32))
    row_top, row_total = lax.fori_loop(0, last_block, lse_step, start_pair)
    return row_top + jnp.log(row_total)


def attend_rows(queries, kv_all, row_lse, key_width, offset, last_block):

    def out_step(key_block, accumulated):
        scores, key_rows, value_rows = block_scores(queries, kv_all, key_block, key_width, offset)
        attn_probs = jnp.exp(scores - row_lse[..., None]).astype(jnp.bfloat16)
        return accumulated + jnp.einsum(
            "hqk,khd->qhd", attn_probs, value_rows, preferred_element_type=jnp.float32
        )

    accumulated = lax.fori_loop(0, last_block, out_step, jnp.zeros(queries.shape, jnp.float32))
    return accumulated.reshape(queries.shape[0], -1).astype(jnp.bfloat16)


def delta_rows(queries, kv_all, row_lse, grad_rows, key_width, offset, last_block):

    def delta_step(key_block, row_delta):
        scores, key_rows, value_rows = block_scores(queries, kv_all, key_block, key_width, offset)
        plain_probs = jnp.exp(scores - row_lse[..., None])
        prob_grad = jnp.einsum(
            "qhd,khd->hqk", grad_rows, value_rows, preferred_element_type=jnp.float32
        )
        return row_delta + jnp.sum(plain_probs * prob_grad, axis=-1)

    return lax.fori_loop(0, last_block, delta_step, jnp.zeros(row_lse.shape, jnp.float32))


def attend_back(
    queries, kv_all, row_lse, row_delta, grad_rows, key_width, offset, last_block, length
):
    model_width = queries.shape[1] * queries.shape[2]

    def grad_step(key_block, state_pair):
        query_grad, kv_grad = state_pair
        scores, key_rows, value_rows = block_scores(queries, kv_all, key_block, key_width, offset)
        plain_probs = jnp.exp(scores - row_lse[..., None])
        prob_grad = jnp.einsum(
            "qhd,khd->hqk", grad_rows, value_rows, preferred_element_type=jnp.float32
        )
        score_grad = (plain_probs * (prob_grad - row_delta[..., None])).astype(jnp.bfloat16)
        query_grad = query_grad + jnp.einsum(
            "hqk,khd->qhd", score_grad, key_rows, preferred_element_type=jnp.float32
        )
        key_grad = (
            jnp.einsum("hqk,qhd->khd", score_grad, queries, preferred_element_type=jnp.float32)
            * 0.125
        )
        value_grad = jnp.einsum(
            "hqk,qhd->khd",
            plain_probs.astype(jnp.bfloat16),
            grad_rows,
            preferred_element_type=jnp.float32,
        )
        kv_piece = jnp.concatenate(
            [key_grad.reshape(key_width, -1), value_grad.reshape(key_width, -1)], axis=1
        )
        kv_grad = lax.dynamic_update_slice_in_dim(kv_grad, kv_piece, key_block * key_width, 0)
        return (query_grad, kv_grad)

    start_pair = (
        jnp.zeros(queries.shape, jnp.float32),
        jnp.zeros((length, 2 * model_width), jnp.float32),
    )
    query_grad, kv_grad = lax.fori_loop(0, last_block, grad_step, start_pair)
    return (query_grad.reshape(queries.shape[0], -1) * 0.125, kv_grad)


def per_device(
    patches,
    w_in,
    b_in,
    g_one,
    s_one,
    w_qkv,
    w_out,
    b_out,
    g_two,
    s_two,
    w_up,
    b_up,
    w_down,
    b_down,
    cotangent,
):
    shards = (
        w_in,
        b_in,
        g_one,
        s_one,
        w_qkv,
        w_out,
        b_out,
        g_two,
        s_two,
        w_up,
        b_up,
        w_down,
        b_down,
    )
    micro_count = patches.shape[0]
    row_count = patches.shape[1]
    model_width = w_qkv.shape[1] // 3
    all_devices = lax.axis_size(("dp", "ctx"))
    length = row_count * lax.axis_size("ctx")
    key_width = min(512, length)
    offset = lax.axis_index("ctx") * row_count
    last_block = (offset + row_count - 1) // key_width + 1
    totals = [
        jnp.zeros((shard.shape[0] * all_devices,) + shard.shape[1:], jnp.float32)
        for shard in shards
    ]
    outputs = []
    in_grads = []
    for batch_index in range(micro_count):
        gathered = (
            lax.all_gather(w_in, ("dp", "ctx"), axis=0, tiled=True),
            lax.all_gather(b_in, ("dp", "ctx"), axis=0, tiled=True),
            lax.all_gather(g_one, ("dp", "ctx"), axis=0, tiled=True),
            lax.all_gather(s_one, ("dp", "ctx"), axis=0, tiled=True),
            lax.all_gather(w_qkv, ("dp", "ctx"), axis=0, tiled=True),
            lax.all_gather(w_out, ("dp", "ctx"), axis=0, tiled=True),
            lax.all_gather(b_out, ("dp", "ctx"), axis=0, tiled=True),
            lax.all_gather(g_two, ("dp", "ctx"), axis=0, tiled=True),
            lax.all_gather(s_two, ("dp", "ctx"), axis=0, tiled=True),
            lax.all_gather(w_up, ("dp", "ctx"), axis=0, tiled=True),
            lax.all_gather(b_up, ("dp", "ctx"), axis=0, tiled=True),
            lax.all_gather(w_down, ("dp", "ctx"), axis=0, tiled=True),
            lax.all_gather(b_down, ("dp", "ctx"), axis=0, tiled=True),
        )
        seq_patches = patches[batch_index]
        h_zero = jnp.dot(seq_patches, gathered[0], preferred_element_type=jnp.float32) + gathered[
            1
        ].astype(jnp.float32)
        gain_one = gathered[2].astype(jnp.float32)
        n_one, normed_one, inverse_one = norm_forward(
            h_zero, gain_one, gathered[3].astype(jnp.float32)
        )
        a_one = n_one.astype(jnp.bfloat16)
        projected = jnp.dot(a_one, gathered[4], preferred_element_type=jnp.float32).astype(
            jnp.bfloat16
        )
        queries = projected[:, :model_width].reshape(row_count, HEADS, HEAD)
        kv_all = lax.all_gather(projected[:, model_width:], "ctx", axis=0, tiled=True)
        row_lse = log_totals(queries, kv_all, key_width, offset, last_block)
        attended = attend_rows(queries, kv_all, row_lse, key_width, offset, last_block)
        h_one = (
            h_zero
            + jnp.dot(attended, gathered[5], preferred_element_type=jnp.float32)
            + gathered[6].astype(jnp.float32)
        )
        gain_two = gathered[7].astype(jnp.float32)
        n_two, normed_two, inverse_two = norm_forward(
            h_one, gain_two, gathered[8].astype(jnp.float32)
        )
        a_two = n_two.astype(jnp.bfloat16)
        pre_act = jnp.dot(a_two, gathered[9], preferred_element_type=jnp.float32) + gathered[
            10
        ].astype(jnp.float32)
        gelu_out, gelu_slope = gelu_pair(pre_act)
        hidden = gelu_out.astype(jnp.bfloat16)
        result = (
            h_one
            + jnp.dot(hidden, gathered[11], preferred_element_type=jnp.float32)
            + gathered[12].astype(jnp.float32)
        )
        outputs.append(result.astype(jnp.bfloat16))
        back_weights = (
            lax.all_gather(w_in, ("dp", "ctx"), axis=0, tiled=True),
            lax.all_gather(b_in, ("dp", "ctx"), axis=0, tiled=True),
            lax.all_gather(g_one, ("dp", "ctx"), axis=0, tiled=True),
            lax.all_gather(s_one, ("dp", "ctx"), axis=0, tiled=True),
            lax.all_gather(w_qkv, ("dp", "ctx"), axis=0, tiled=True),
            lax.all_gather(w_out, ("dp", "ctx"), axis=0, tiled=True),
            lax.all_gather(b_out, ("dp", "ctx"), axis=0, tiled=True),
            lax.all_gather(g_two, ("dp", "ctx"), axis=0, tiled=True),
            lax.all_gather(s_two, ("dp", "ctx"), axis=0, tiled=True),
            lax.all_gather(w_up, ("dp", "ctx"), axis=0, tiled=True),
            lax.all_gather(b_up, ("dp", "ctx"), axis=0, tiled=True),
            lax.all_gather(w_down, ("dp", "ctx"), axis=0, tiled=True),
            lax.all_gather(b_down, ("dp", "ctx"), axis=0, tiled=True),
        )
        seq_cot = cotangent[batch_index]
        cot_float = seq_cot.astype(jnp.float32)
        totals[12] = totals[12] + jnp.sum(cot_float, axis=0)
        totals[11] = totals[11] + jnp.dot(hidden.T, seq_cot, preferred_element_type=jnp.float32)
        pre_grad = (
            jnp.dot(seq_cot, back_weights[11].T, preferred_element_type=jnp.float32) * gelu_slope
        )
        totals[10] = totals[10] + jnp.sum(pre_grad, axis=0)
        up_grad = pre_grad.astype(jnp.bfloat16)
        totals[9] = totals[9] + jnp.dot(a_two.T, up_grad, preferred_element_type=jnp.float32)
        two_grad = jnp.dot(up_grad, back_weights[9].T, preferred_element_type=jnp.float32)
        norm_grad, gain_grad, shift_grad = norm_backward(
            two_grad, normed_two, inverse_two, back_weights[7].astype(jnp.float32)
        )
        totals[7] = totals[7] + gain_grad
        totals[8] = totals[8] + shift_grad
        stream_one = cot_float + norm_grad
        totals[6] = totals[6] + jnp.sum(stream_one, axis=0)
        out_grad = stream_one.astype(jnp.bfloat16)
        totals[5] = totals[5] + jnp.dot(attended.T, out_grad, preferred_element_type=jnp.float32)
        attended_grad = jnp.dot(
            out_grad, back_weights[5].T, preferred_element_type=jnp.float32
        ).astype(jnp.bfloat16)
        grad_rows = attended_grad.reshape(row_count, HEADS, HEAD)
        row_delta = delta_rows(queries, kv_all, row_lse, grad_rows, key_width, offset, last_block)
        query_grad, kv_terms = attend_back(
            queries, kv_all, row_lse, row_delta, grad_rows, key_width, offset, last_block, length
        )
        kv_local = lax.psum_scatter(
            kv_terms.astype(jnp.bfloat16), "ctx", scatter_dimension=0, tiled=True
        ).astype(jnp.float32)
        projected_grad = jnp.concatenate([query_grad, kv_local], axis=1).astype(jnp.bfloat16)
        totals[4] = totals[4] + jnp.dot(a_one.T, projected_grad, preferred_element_type=jnp.float32)
        one_grad = jnp.dot(projected_grad, back_weights[4].T, preferred_element_type=jnp.float32)
        norm_grad, gain_grad, shift_grad = norm_backward(
            one_grad, normed_one, inverse_one, back_weights[2].astype(jnp.float32)
        )
        totals[2] = totals[2] + gain_grad
        totals[3] = totals[3] + shift_grad
        stream_zero = stream_one + norm_grad
        totals[1] = totals[1] + jnp.sum(stream_zero, axis=0)
        zero_grad = stream_zero.astype(jnp.bfloat16)
        totals[0] = totals[0] + jnp.dot(
            seq_patches.T, zero_grad, preferred_element_type=jnp.float32
        )
        in_grads.append(jnp.dot(zero_grad, back_weights[0].T, preferred_element_type=jnp.float32))
    owned = (
        lax.psum_scatter(totals[0], ("dp", "ctx"), scatter_dimension=0, tiled=True),
        lax.psum_scatter(totals[1], ("dp", "ctx"), scatter_dimension=0, tiled=True),
        lax.psum_scatter(totals[2], ("dp", "ctx"), scatter_dimension=0, tiled=True),
        lax.psum_scatter(totals[3], ("dp", "ctx"), scatter_dimension=0, tiled=True),
        lax.psum_scatter(totals[4], ("dp", "ctx"), scatter_dimension=0, tiled=True),
        lax.psum_scatter(totals[5], ("dp", "ctx"), scatter_dimension=0, tiled=True),
        lax.psum_scatter(totals[6], ("dp", "ctx"), scatter_dimension=0, tiled=True),
        lax.psum_scatter(totals[7], ("dp", "ctx"), scatter_dimension=0, tiled=True),
        lax.psum_scatter(totals[8], ("dp", "ctx"), scatter_dimension=0, tiled=True),
        lax.psum_scatter(totals[9], ("dp", "ctx"), scatter_dimension=0, tiled=True),
        lax.psum_scatter(totals[10], ("dp", "ctx"), scatter_dimension=0, tiled=True),
        lax.psum_scatter(totals[11], ("dp", "ctx"), scatter_dimension=0, tiled=True),
        lax.psum_scatter(totals[12], ("dp", "ctx"), scatter_dimension=0, tiled=True),
    )
    return (jnp.stack(outputs), jnp.stack(in_grads)) + tuple(owned)


def solution(mesh):
    placed = (
        P("dp", "ctx", None),
        P(("dp", "ctx"), None),
        P(("dp", "ctx")),
        P(("dp", "ctx")),
        P(("dp", "ctx")),
        P(("dp", "ctx"), None),
        P(("dp", "ctx"), None),
        P(("dp", "ctx")),
        P(("dp", "ctx")),
        P(("dp", "ctx")),
        P(("dp", "ctx"), None),
        P(("dp", "ctx")),
        P(("dp", "ctx"), None),
        P(("dp", "ctx")),
        P("dp", "ctx", None),
    )
    return jax.shard_map(
        per_device,
        mesh=mesh,
        in_specs=placed,
        out_specs=(
            P("dp", "ctx", None),
            P("dp", "ctx", None),
            P(("dp", "ctx"), None),
            P(("dp", "ctx")),
            P(("dp", "ctx")),
            P(("dp", "ctx")),
            P(("dp", "ctx"), None),
            P(("dp", "ctx"), None),
            P(("dp", "ctx")),
            P(("dp", "ctx")),
            P(("dp", "ctx")),
            P(("dp", "ctx"), None),
            P(("dp", "ctx")),
            P(("dp", "ctx"), None),
            P(("dp", "ctx")),
        ),
        check_vma=False,
    )
```

profile of v0, /device:TPU:0, one launch (start us, length us, event | category | flops | bytes accessed | tf_op | source)
XLA Modules:
  0.0 1311.8 jit_solution(26952344656384240)
XLA Ops:
  15.4 42.9 %all-reduce.17 = (bf16[768]{0:T(1024)(128)(2,1)S(1)}, bf16[768]{0:T(1024)(128)(2,1)S(1)}, bf16[768]{0:T(1024)(128)(2,1)S(1)}, bf16[768]{0:T(1024)(128)(2,1)}, bf...) all-reduce(bf16[768]{0:T(1024)(128)(2,1)S(1)} %dynamic-update-slice, ...), channel_id=1, replica_groups=mesh['dp'=4,'ctx'=8] {'dp','ctx'}, use_global_device_ids=true, to_apply=%add | all-reduce | flops 8448 | bytes 33792
  58.3 37.5 %all-gather.8.cloned.1.call-done = bf16[6144,768]{1,0:T(8,128)(2,1)} async-done(((bf16[192,768]{1,0:T(8,128)(2,1)}), bf16[6144,768]{1,0:T(8,128)(2,1)}) %all-gather.8.cloned.1.call-update) | async-done | bytes 9437200 | tf_op jit(solution)/shard_map/all_gather | solution.py:183
  95.8 5.6 fusion.127
  101.7 55.7 %all-gather.10.cloned.1.call-done = bf16[768,2304]{1,0:T(8,128)(2,1)} async-done(((bf16[24,2304]{1,0:T(8,128)(2,1)}), bf16[768,2304]{1,0:T(8,128)(2,1)}) %all-gather.10.cloned.1.call-update) | async-done | bytes 3538960 | tf_op jit(solution)/shard_map/all_gather | solution.py:187
  157.4 2.7 convolution_convert_fusion.1
  161.7 5.8 fusion.125
  177.6 15.4 %all-gather.12.cloned.1.call-done = bf16[1024,1536]{1,0:T(8,128)(2,1)} async-done(((bf16[128,1536]{1,0:T(8,128)(2,1)}), bf16[1024,1536]{1,0:T(8,128)(2,1)}) %all-gather.12.cloned.1.call-update) | async-done | bytes 3145744 | tf_op jit(solution)/shard_map/all_gather | solution.py:210
  193.0 3.2 copy.86
  201.2 5.6 while.89
  203.3 3.5 fusion.267
  208.5 18.6 %all-gather.20.cloned.1.call-done = bf16[1024,1536]{1,0:T(8,128)(2,1)} async-done(((bf16[128,1536]{1,0:T(8,128)(2,1)}), bf16[1024,1536]{1,0:T(8,128)(2,1)}) %all-gather.20.cloned.1.call-update) | async-done | bytes 3145744 | tf_op jit(solution)/shard_map/all_gather | solution.py:210
  227.1 4.6 copy.89
  232.3 3.7 while.90
  238.1 7.0 while.91
  238.9 2.7 constant_dynamic-slice_fusion.15
  241.5 3.5 fusion.274
  246.8 37.1 %all-gather.14.cloned.1.call-done = bf16[768,768]{1,0:T(8,128)(2,1)} async-done(((bf16[24,768]{1,0:T(8,128)(2,1)}), bf16[768,768]{1,0:T(8,128)(2,1)}) %all-gather.14.cloned.1.call-update) | async-done | bytes 1179664 | tf_op jit(solution)/shard_map/all_gather | solution.py:188
  289.6 59.6 %all-gather.16.cloned.1.call-done = bf16[768,3072]{1,0:T(8,128)(2,1)} async-done(((bf16[24,3072]{1,0:T(8,128)(2,1)}), bf16[768,3072]{1,0:T(8,128)(2,1)}) %all-gather.16.cloned.1.call-update) | async-done | bytes 4718608 | tf_op jit(solution)/shard_map/all_gather | solution.py:192
  349.2 4.5 convolution_add_fusion.3
  353.7 60.9 %all-gather.18.cloned.1.call-done = bf16[3072,768]{1,0:T(8,128)(2,1)} async-done(((bf16[96,768]{1,0:T(8,128)(2,1)}), bf16[3072,768]{1,0:T(8,128)(2,1)}) %all-gather.18.cloned.1.call-update) | async-done | bytes 4718608 | tf_op jit(solution)/shard_map/all_gather | solution.py:194
  414.6 5.5 fusion.130
  423.7 2.5 fusion.129
  434.0 2.6 convolution_convert_fusion.2
  438.4 3.6 while.94
  442.6 11.3 while.92
  456.8 7.4 while.93
  464.3 4.7 copy.105
  471.9 7.4 while.95
  479.3 4.6 copy.107
  489.4 5.5 convolution_add_fusion.1
  497.8 5.0 convolution_add_fusion.2
  504.2 23.9 %reduce-scatter.22.cloned.1.call-done = bf16[128,1536]{1,0:T(8,128)(2,1)} async-done(((bf16[1024,1536]{1,0:T(8,128)(2,1)}), bf16[128,1536]{1,0:T(8,128)(2,1)}) %reduce-scatter.22.cloned.1.call-update) | async-done | bytes 393232
  529.3 49.4 %reduce-scatter.24.cloned.1.call-done = bf16[128,1536]{1,0:T(8,128)(2,1)} async-done(((bf16[1024,1536]{1,0:T(8,128)(2,1)}), bf16[128,1536]{1,0:T(8,128)(2,1)}) %reduce-scatter.24.cloned.1.call-update) | async-done | bytes 393232
  581.3 4.1 convolution_add_fusion
  587.5 3.4 multiply_reduce_fusion.3
  593.0 8.1 fusion.63
  601.1 12.6 add_bitcast_fusion
  613.7 18.7 %copy.109 = f32[6144,768]{1,0:T(8,128)} copy(f32[6144,768]{0,1:T(8,128)} %add_bitcast_fusion) | data formatting | bytes 37748736
  634.0 3.5 fusion.83
  637.6 3.5 fusion.84
  642.0 40.9 %all-reduce.16 = (f32[768]{0:T(1024)S(1)}, f32[768]{0:T(1024)S(1)}, f32[768]{0:T(1024)S(1)}, f32[768]{0:T(1024)S(1)}, f32[768]{0:T(1024)S(1)}, /*index=5*/f32[76...) all-reduce(f32[768]{0:T(1024)S(1)} %add.529, ...), channel_id=5, replica_groups=mesh['dp'=4,'ctx'=8] {'dp','ctx'}, use_global_device_ids=true, to_apply=%region_43.44.clone | all-reduce | flops 8448 | bytes 67584
  687.6 6.9 convolution_bitcast_fusion.2
  694.5 3.1 convolution_bitcast_fusion.3
  697.6 3.1 pad_maximum_fusion
  700.8 125.0 %reduce-scatter.20.cloned.1.call-done = f32[96,768]{1,0:T(8,128)} async-done(((f32[3072,768]{1,0:T(8,128)}), f32[96,768]{1,0:T(8,128)}) %reduce-scatter.20.cloned.1.call-update) | async-done | bytes 294928 | tf_op jit(solution)/shard_map/reduce_scatter | solution.py:307
  825.8 140.9 %reduce-scatter.18.cloned.1.call-done = f32[24,3072]{1,0:T(8,128)} async-done(((f32[768,3072]{1,0:T(8,128)}), f32[24,3072]{1,0:T(8,128)}) %reduce-scatter.18.cloned.1.call-update) | async-done | bytes 294928 | tf_op jit(solution)/shard_map/reduce_scatter | solution.py:305
  966.7 125.3 %reduce-scatter.14.cloned.1.call-done = f32[24,2304]{1,0:T(8,128)} async-done(((f32[768,2304]{1,0:T(8,128)}), f32[24,2304]{1,0:T(8,128)}) %reduce-scatter.14.cloned.1.call-update) | async-done | bytes 221200 | tf_op jit(solution)/shard_map/reduce_scatter | solution.py:300
  1092.0 212.8 %reduce-scatter.26.cloned.1.call-done = f32[192,768]{1,0:T(8,128)} async-done(((f32[6144,768]{1,0:T(8,128)}), f32[192,768]{1,0:T(8,128)}) %reduce-scatter.26.cloned.1.call-update) | async-done | bytes 589840
  (431 shorter events, 109.9 us)
Async XLA Ops:
  7.2 88.6 %all-gather.8.cloned.1.call-start = ((), (), s32[]{:S(2)}) async-start(), calls=%async_computation.7 | async-start | bytes 9732096 | tf_op jit(solution)/shard_map/all_gather | solution.py:183
  7.9 149.5 %all-gather.10.cloned.1.call-start = ((), (), s32[]{:S(2)}) async-start(), calls=%async_computation.8 | async-start | bytes 3649536 | tf_op jit(solution)/shard_map/all_gather | solution.py:187
  8.7 184.3 %all-gather.12.cloned.1.call-start = ((), (), s32[]{:S(2)}) async-start(), calls=%async_computation.9 | async-start | bytes 3538944 | tf_op jit(solution)/shard_map/all_gather | solution.py:210
  58.3 109.4 %copy-start.59 = (f32[768]{0:T(1024)}, f32[768]{0:T(1024)S(1)}, u32[]{:S(2)}) copy-start(f32[768]{0:T(1024)S(1)} %convert_element_type.137) | copy-start | bytes 9220
  58.3 109.4 %copy-start.68 = (f32[768]{0:T(1024)}, f32[768]{0:T(1024)S(1)}, u32[]{:S(2)}) copy-start(f32[768]{0:T(1024)S(1)} %convert_element_type.138) | copy-start | bytes 9220
  101.4 60.2 %copy-start.16 = (f32[128,768]{1,0:T(8,128)}, f32[128,768]{1,0:T(8,128)S(1)}, u32[]{:S(2)}) copy-start(f32[128,768]{1,0:T(8,128)S(1)} %get-tuple-element.817) | copy-start | bytes 1179652
  101.4 60.2 %copy-start.93 = (f32[128]{0:T(128)}, f32[128]{0:T(128)S(1)}, u32[]{:S(2)}) copy-start(f32[128]{0:T(128)S(1)} %broadcast_multiply_fusion.11) | copy-start | bytes 1540
  101.7 60.0 %copy-start.108 = (f32[128]{0:T(128)}, f32[128]{0:T(128)S(1)}, u32[]{:S(2)}) copy-start(f32[128]{0:T(128)S(1)} %add_rsqrt_fusion.3) | copy-start | bytes 1540
  161.7 6.1 copy-start.2
  161.7 65.4 %all-gather.20.cloned.1.call-start = ((), (), s32[]{:S(2)}) async-start(), calls=%async_computation.13 | async-start | bytes 3538944 | tf_op jit(solution)/shard_map/all_gather | solution.py:210
  170.2 113.7 %all-gather.14.cloned.1.call-start = ((), (), s32[]{:S(2)}) async-start(), calls=%async_computation.10 | async-start | bytes 1216512 | tf_op jit(solution)/shard_map/all_gather | solution.py:188
  170.7 178.5 %all-gather.16.cloned.1.call-start = ((), (), s32[]{:S(2)}) async-start(), calls=%async_computation.11 | async-start | bytes 4866048 | tf_op jit(solution)/shard_map/all_gather | solution.py:192
  171.3 243.3 %all-gather.18.cloned.1.call-start = ((), (), s32[]{:S(2)}) async-start(), calls=%async_computation.12 | async-start | bytes 4866048 | tf_op jit(solution)/shard_map/all_gather | solution.py:194
  172.1 356.0 %reduce-scatter.22.cloned.1.call-start = ((), (), s32[]{:S(2)}) async-start(), calls=%async_computation.18 | async-start | bytes 3538944
  238.1 45.8 %copy-start.75 = (f32[768]{0:T(1024)S(1)}, f32[768]{0:T(1024)}, u32[]{:S(2)}) copy-start(f32[768]{0:T(1024)} %convert_element_type.143) | copy-start | bytes 9220
  285.9 142.7 %copy-start.76 = (f32[128]{0:T(128)}, f32[128]{0:T(128)S(1)}, u32[]{:S(2)}) copy-start(f32[128]{0:T(128)S(1)} %broadcast_multiply_fusion.10) | copy-start | bytes 1540
  287.7 140.9 %copy-start.86 = (f32[128]{0:T(128)}, f32[128]{0:T(128)S(1)}, u32[]{:S(2)}) copy-start(f32[128]{0:T(128)S(1)} %broadcast_multiply_fusion.8) | copy-start | bytes 1540
  414.6 6.4 copy-start.1
  414.6 9.0 slice-start.3
  469.0 109.7 %reduce-scatter.24.cloned.1.call-start = ((), (), s32[]{:S(2)}) async-start(), calls=%async_computation.19 | async-start | bytes 3538944
  484.0 216.8 %reduce-scatter.16.cloned.1.call-start = ((), (), s32[]{:S(2)}) async-start(), calls=%async_computation.15 | async-start | bytes 2433024 | tf_op jit(solution)/shard_map/reduce_scatter | solution.py:301
  487.6 338.2 %reduce-scatter.20.cloned.1.call-start = ((), (), s32[]{:S(2)}) async-start(), calls=%async_computation.17 | async-start | bytes 9732096 | tf_op jit(solution)/shard_map/reduce_scatter | solution.py:307
  495.0 471.7 %reduce-scatter.18.cloned.1.call-start = ((), (), s32[]{:S(2)}) async-start(), calls=%async_computation.16 | async-start | bytes 9732096 | tf_op jit(solution)/shard_map/reduce_scatter | solution.py:305
  502.8 77.1 %copy-start.60 = (f32[768]{0:T(1024)S(1)}, f32[768]{0:T(1024)}, u32[]{:S(2)}) copy-start(f32[768]{0:T(1024)} %copy-done.59) | copy-start | bytes 9220
  502.8 77.1 %copy-start.69 = (f32[768]{0:T(1024)S(1)}, f32[768]{0:T(1024)}, u32[]{:S(2)}) copy-start(f32[768]{0:T(1024)} %copy-done.68) | copy-start | bytes 9220
  502.8 77.1 %copy-start.94 = (f32[128]{0:T(128)S(1)}, f32[128]{0:T(128)}, u32[]{:S(2)}) copy-start(f32[128]{0:T(128)} %copy-done.93) | copy-start | bytes 1540
  502.8 77.1 %copy-start.109 = (f32[128]{0:T(128)S(1)}, f32[128]{0:T(128)}, u32[]{:S(2)}) copy-start(f32[128]{0:T(128)} %copy-done.108) | copy-start | bytes 1540
  502.9 77.1 %copy-start.17 = (f32[128,768]{1,0:T(8,128)S(1)}, f32[128,768]{1,0:T(8,128)}, u32[]{:S(2)}) copy-start(f32[128,768]{1,0:T(8,128)} %copy-done.16) | copy-start | bytes 1179652
  502.9 589.1 %reduce-scatter.14.cloned.1.call-start = ((), (), s32[]{:S(2)}) async-start(), calls=%async_computation.14 | async-start | bytes 7299072 | tf_op jit(solution)/shard_map/reduce_scatter | solution.py:300
  504.0 77.3 %copy-start.58 = (bf16[128,12,64]{0,2,1:T(8,128)(2,1)}, bf16[128,12,64]{0,2,1:T(8,128)(2,1)S(1)}, u32[]{:S(2)}) copy-start(bf16[128,12,64]{0,2,1:T(8,128)(2,1)S(1)} %multiply_convert_fusion.3) | copy-start | bytes 589828
  504.2 77.1 %copy-start.51 = (bf16[128,12,64]{0,2,1:T(8,128)(2,1)}, bf16[128,12,64]{0,2,1:T(8,128)(2,1)S(1)}, u32[]{:S(2)}) copy-start(bf16[128,12,64]{0,2,1:T(8,128)(2,1)S(1)} %multiply_convert_fusion.2) | copy-start | bytes 589828
  529.3 52.0 %copy-start.57 = (bf16[128,1536]{0,1:T(8,128)(2,1)}, bf16[128,1536]{0,1:T(8,128)(2,1)S(1)}, u32[]{:S(2)}) copy-start(bf16[128,1536]{0,1:T(8,128)(2,1)S(1)} %copy.106) | copy-start | bytes 1179652
  585.5 719.4 %reduce-scatter.26.cloned.1.call-start = ((), (), s32[]{:S(2)}) async-start(), calls=%async_computation.20 | async-start | bytes 19464192
  587.4 3.4 copy-start.42
  587.4 3.4 copy-start.52
  587.5 3.4 copy-start.90
  587.5 3.4 copy-start.95
  587.5 3.4 copy-start.102
  587.5 3.4 copy-start.110
  592.4 8.7 copy-start.47
  634.0 3.5 copy-start.22
  634.0 3.5 copy-start.33
  637.6 4.3 copy-start.112
  637.6 4.3 copy-start.111
  637.6 56.9 %slice-start = ((s8[9437184]{0:T(1024)(128)(4,1)}), s8[1048576]{0:T(1024)(128)(4,1)S(1)}, s32[]{:S(2)}) async-start(s8[9437184]{0:T(1024)(128)(4,1)} %bitcast.411), calls=%async_computation.21 | async-start | bytes 2097152
  687.6 6.9 slice-start.1
  687.6 6.9 slice-start.2
  687.6 7.0 copy-start.48
  (85 other events, 130.3 us)
Sparse Core Ops, SparseCore 0:
  10.9 84.8 all-gather.7
  98.7 58.6 all-gather.9
  161.8 31.1 all-gather.11
  194.7 32.3 all-gather.19
  229.8 54.0 all-gather.13
  286.6 62.5 all-gather.15
  352.1 62.4 all-gather.17
  469.1 58.9 reduce-scatter.21
  532.4 46.2 reduce-scatter.23
  584.4 99.1 reduce-scatter.15
  691.0 134.6 reduce-scatter.19
  832.1 134.5 reduce-scatter.17
  973.9 118.0 reduce-scatter.13
  1098.8 205.9 reduce-scatter.25
where the time goes:
time: 1320 us; the launch traced here: 1310 us
  waiting for transfers between devices  965 us (73%)
  matrix products  124 us (9%)
  local copies, waits for them, and re-layouts  91.7 us (7%)
  blocking collectives  83.8 us (6%)
  other arithmetic  21.3 us (2%)
  between operations  15.7 us (1%)
    unnamed x17, waiting for transfers between devices  289 us
    reduce_scatter x1, waiting for transfers between devices, per_device(): lax.psum_scatter(totals[9], ('dp', 'ctx'), scatter_dimension=0, tiled=True)  141 us
    reduce_scatter x1, waiting for transfers between devices, per_device(): lax.psum_scatter(totals[4], ('dp', 'ctx'), scatter_dimension=0, tiled=True)  125 us
    reduce_scatter x1, waiting for transfers between devices, per_device(): lax.psum_scatter(totals[11], ('dp', 'ctx'), scatter_dimension=0, tiled=True)  125 us
    unnamed x2, blocking collectives  83.8 us
    all_gather x1, waiting for transfers between devices, per_device(): lax.all_gather(w_down, ('dp', 'ctx'), axis=0, tiled=True)  60.9 us
    all_gather x1, waiting for transfers between devices, per_device(): lax.all_gather(w_up, ('dp', 'ctx'), axis=0, tiled=True)  59.6 us
    all_gather x1, waiting for transfers between devices, per_device(): lax.all_gather(w_qkv, ('dp', 'ctx'), axis=0, tiled=True)  55.7 us
  transfers between devices with their start and end apart: 14, of which 13 were waited for; matrix products, arithmetic and copies ran while one was open for 13% of the time, Pallas kernels for 0%

commit v1 on v0

--- a/solution.py
+++ b/solution.py
@@ -7,6 +7,19 @@
 HEAD = 64
 eps_norm = 1e-05
 gelu_coef = 0.7978845608028654
+
+
+def ring_gather(array, axis, dim):
+    ways = lax.axis_size(axis)
+    up = [(d, (d + 1) % ways) for d in range(ways)]
+    down = [(d, (d - 1) % ways) for d in range(ways)]
+    earlier, later = ([array], [array])
+    for _ in range(ways // 2):
+        earlier.append(lax.ppermute(earlier[-1], axis, up))
+    for _ in range((ways - 1) // 2):
+        later.append(lax.ppermute(later[-1], axis, down))
+    line = jnp.concatenate([*earlier[::-1], *later[1:]], axis=dim)
+    return jnp.roll(line, (lax.axis_index(axis) - ways // 2) * array.shape[dim], axis=dim)
 
 
 def norm_forward(stream, gain, shift):
@@ -207,7 +220,7 @@
             jnp.bfloat16
         )
         queries = projected[:, :model_width].reshape(row_count, HEADS, HEAD)
-        kv_all = lax.all_gather(projected[:, model_width:], "ctx", axis=0, tiled=True)
+        kv_all = ring_gather(projected[:, model_width:], "ctx", 0)
         row_lse = log_totals(queries, kv_all, key_width, offset, last_block)
         attended = attend_rows(queries, kv_all, row_lse, key_width, offset, last_block)
         h_one = (

time: 1320 us -> 1250 us (0.947)
  waiting for transfers between devices: 965 us -> 873 us
  starting transfers between devices: 1.03 us -> 15.4 us
    all_gather x1, waiting for transfers between devices: 59.6 us -> 0.01 us  [per_device(): lax.all_gather(w_up, ('dp', 'ctx'), axis=0, tiled=True)]
    ppermute x0 -> x14, waiting for transfers between devices: none -> 43.8 us  [the longest x8 42.4 us: ring_gather(): earlier.append(lax.ppermute(earlier[-1], axis, up))]
    all_gather x1, waiting for transfers between devices: 37.1 us -> 0.01 us  [per_device(): lax.all_gather(w_out, ('dp', 'ctx'), axis=0, tiled=True)]
    all_gather x2 -> x0, waiting for transfers between devices: 33.9 us -> none  [per_device(): lax.all_gather(projected[:, model_width:], 'ctx', axis=0, tiled=True)]
    ppermute x0 -> x14, starting transfers between devices: none -> 14.5 us  [the longest x6 12.4 us: ring_gather(): later.append(lax.ppermute(later[-1], axis, down))]
    unnamed x219 -> x249, local copies, waits for them, and re-layouts: 53 us -> 60.7 us
    unnamed x17 -> x15, waiting for transfers between devices: 289 us -> 289 us
  transfers between devices with their start and end apart: 14 -> 26, of which waited for: 13 -> 17; matrix products, arithmetic and copies ran while one was open for 13% -> 15% of each run, Pallas kernels for 0% -> 0%
where the time goes in v1:
time: 1250 us; the launch traced here: 1240 us
  waiting for transfers between devices  873 us (70%)
  matrix products  124 us (10%)
  local copies, waits for them, and re-layouts  97.5 us (8%)
  blocking collectives  83.8 us (7%)
  other arithmetic  26 us (2%)
  between operations  16.3 us (1%)
  starting transfers between devices  15.4 us (1%)
    unnamed x15, waiting for transfers between devices  289 us
    reduce_scatter x1, waiting for transfers between devices, per_device(): lax.psum_scatter(totals[9], ('dp', 'ctx'), scatter_dimension=0, tiled=True)  141 us
    reduce_scatter x1, waiting for transfers between devices, per_device(): lax.psum_scatter(totals[4], ('dp', 'ctx'), scatter_dimension=0, tiled=True)  126 us
    reduce_scatter x1, waiting for transfers between devices, per_device(): lax.psum_scatter(totals[11], ('dp', 'ctx'), scatter_dimension=0, tiled=True)  125 us
    unnamed x2, blocking collectives  83.8 us
    unnamed x249, local copies, waits for them, and re-layouts  60.7 us
    all_gather x1, waiting for transfers between devices, per_device(): lax.all_gather(w_down, ('dp', 'ctx'), axis=0, tiled=True)  57.5 us
    all_gather x1, waiting for transfers between devices, per_device(): lax.all_gather(w_qkv, ('dp', 'ctx'), axis=0, tiled=True)  55.2 us
  transfers between devices with their start and end apart: 26, of which 17 were waited for; matrix products, arithmetic and copies ran while one was open for 15% of the time, Pallas kernels for 0%

profile of v1, /device:TPU:0, one launch (start us, length us, event | category | flops | bytes accessed | tf_op | source)
XLA Modules:
  0.0 1236.8 jit_solution(15776163148886046769)
XLA Ops:
  16.8 42.9 %all-reduce.17 = (bf16[768]{0:T(1024)(128)(2,1)S(1)}, bf16[768]{0:T(1024)(128)(2,1)S(1)}, bf16[768]{0:T(1024)(128)(2,1)S(1)}, bf16[768]{0:T(1024)(128)(2,1)}, bf...) all-reduce(bf16[768]{0:T(1024)(128)(2,1)S(1)} %dynamic-update-slice, ...), channel_id=1, replica_groups=mesh['dp'=4,'ctx'=8] {'dp','ctx'}, use_global_device_ids=true, to_apply=%add | all-reduce | flops 8448 | bytes 33792
  59.7 35.8 %all-gather.6.cloned.1.call-done = bf16[6144,768]{1,0:T(8,128)(2,1)} async-done(((bf16[192,768]{1,0:T(8,128)(2,1)}), bf16[6144,768]{1,0:T(8,128)(2,1)}) %all-gather.6.cloned.1.call-update) | async-done | bytes 9437200 | tf_op jit(solution)/shard_map/all_gather | solution.py:196
  95.5 5.6 fusion.127
  101.9 55.2 %all-gather.8.cloned.1.call-done = bf16[768,2304]{1,0:T(8,128)(2,1)} async-done(((bf16[24,2304]{1,0:T(8,128)(2,1)}), bf16[768,2304]{1,0:T(8,128)(2,1)}) %all-gather.8.cloned.1.call-update) | async-done | bytes 3538960 | tf_op jit(solution)/shard_map/all_gather | solution.py:200
  157.1 2.7 convolution_convert_fusion
  160.9 5.3 fusion.129
  172.0 6.4 collective-permute-done
  178.4 8.6 collective-permute-done.8
  191.0 2.8 collective-permute-start.12
  196.4 10.0 collective-permute-done.9
  208.2 2.7 collective-permute-start.6
  215.5 8.2 collective-permute-done.10
  227.0 4.1 collective-permute-done.3
  235.4 6.7 fusion.50
  242.1 3.2 copy.89
  250.3 5.6 while.91
  252.4 3.5 fusion.276
  257.7 4.9 copy.86
  263.1 3.4 while.88
  268.7 7.4 while.89
  272.1 3.6 fusion.269
  283.6 4.4 convolution_add_fusion.3
  288.1 57.5 %all-gather.14.cloned.1.call-done = bf16[3072,768]{1,0:T(8,128)(2,1)} async-done(((bf16[96,768]{1,0:T(8,128)(2,1)}), bf16[3072,768]{1,0:T(8,128)(2,1)}) %all-gather.14.cloned.1.call-update) | async-done | bytes 4718608 | tf_op jit(solution)/shard_map/all_gather | solution.py:207
  345.6 5.5 fusion.132
  372.3 4.4 while.92
  379.5 8.6 while.93
  388.1 4.6 copy.105
  395.8 7.4 while.95
  403.2 4.7 copy.107
  413.3 5.7 convolution_add_fusion.1
  421.8 5.1 convolution_add_fusion.2
  428.0 25.1 %reduce-scatter.22.cloned.1.call-done = bf16[128,1536]{1,0:T(8,128)(2,1)} async-done(((bf16[1024,1536]{1,0:T(8,128)(2,1)}), bf16[128,1536]{1,0:T(8,128)(2,1)}) %reduce-scatter.22.cloned.1.call-update) | async-done | bytes 393232
  454.4 48.8 %reduce-scatter.24.cloned.1.call-done = bf16[128,1536]{1,0:T(8,128)(2,1)} async-done(((bf16[1024,1536]{1,0:T(8,128)(2,1)}), bf16[128,1536]{1,0:T(8,128)(2,1)}) %reduce-scatter.24.cloned.1.call-update) | async-done | bytes 393232
  505.7 4.2 convolution_add_fusion
  512.0 3.4 multiply_reduce_fusion.3
  517.5 8.0 fusion.65
  525.6 12.5 %add_bitcast_fusion = f32[6144,768]{0,1:T(8,128)} fusion(f32[768,6144]{1,0:T(8,128)} %fusion.65, bf16[2,128,6144]{2,1,0:T(8,128)(2,1)S(1)} %copy-done.4, bf16[128,768]{1,0:T(8,128)(2,1)S(1)} %get-tuple-element.780), kind=kOutput, calls=%fused_computation.102 | convolution fusion | flops 1212678144 | bytes 39518208 | tf_op jit(solution)/shard_map/dot_general | solution.py:304
  538.0 18.7 %copy.109 = f32[6144,768]{1,0:T(8,128)} copy(f32[6144,768]{0,1:T(8,128)} %add_bitcast_fusion) | data formatting | bytes 37748736
  558.4 3.5 fusion.85
  562.0 3.5 fusion.86
  566.4 40.8 %all-reduce.16 = (f32[768]{0:T(1024)S(1)}, f32[768]{0:T(1024)S(1)}, f32[768]{0:T(1024)S(1)}, f32[768]{0:T(1024)S(1)}, f32[768]{0:T(1024)S(1)}, /*index=5*/f32[76...) all-reduce(f32[768]{0:T(1024)S(1)} %add.538, ...), channel_id=5, replica_groups=mesh['dp'=4,'ctx'=8] {'dp','ctx'}, use_global_device_ids=true, to_apply=%region_43.45.clone | all-reduce | flops 8448 | bytes 67584
  611.9 6.9 convolution_bitcast_fusion.2
  618.9 3.1 convolution_bitcast_fusion.3
  621.9 3.1 pad_maximum_fusion
  625.1 125.2 %reduce-scatter.20.cloned.1.call-done = f32[96,768]{1,0:T(8,128)} async-done(((f32[3072,768]{1,0:T(8,128)}), f32[96,768]{1,0:T(8,128)}) %reduce-scatter.20.cloned.1.call-update) | async-done | bytes 294928 | tf_op jit(solution)/shard_map/reduce_scatter | solution.py:320
  750.3 140.7 %reduce-scatter.18.cloned.1.call-done = f32[24,3072]{1,0:T(8,128)} async-done(((f32[768,3072]{1,0:T(8,128)}), f32[24,3072]{1,0:T(8,128)}) %reduce-scatter.18.cloned.1.call-update) | async-done | bytes 294928 | tf_op jit(solution)/shard_map/reduce_scatter | solution.py:318
  891.0 125.6 %reduce-scatter.14.cloned.1.call-done = f32[24,2304]{1,0:T(8,128)} async-done(((f32[768,2304]{1,0:T(8,128)}), f32[24,2304]{1,0:T(8,128)}) %reduce-scatter.14.cloned.1.call-update) | async-done | bytes 221200 | tf_op jit(solution)/shard_map/reduce_scatter | solution.py:313
  1016.6 212.9 %reduce-scatter.26.cloned.1.call-done = f32[192,768]{1,0:T(8,128)} async-done(((f32[6144,768]{1,0:T(8,128)}), f32[192,768]{1,0:T(8,128)}) %reduce-scatter.26.cloned.1.call-update) | async-done | bytes 589840
  (489 shorter events, 138.3 us)
Async XLA Ops:
  7.2 88.3 %all-gather.6.cloned.1.call-start = ((), (), s32[]{:S(2)}) async-start(), calls=%async_computation.7 | async-start | bytes 9732096 | tf_op jit(solution)/shard_map/all_gather | solution.py:196
  7.9 149.2 %all-gather.8.cloned.1.call-start = ((), (), s32[]{:S(2)}) async-start(), calls=%async_computation.8 | async-start | bytes 3649536 | tf_op jit(solution)/shard_map/all_gather | solution.py:200
  8.7 269.1 %all-gather.10.cloned.1.call-start = ((), (), s32[]{:S(2)}) async-start(), calls=%async_computation.9 | async-start | bytes 1216512 | tf_op jit(solution)/shard_map/all_gather | solution.py:201
  9.4 274.2 %all-gather.12.cloned.1.call-start = ((), (), s32[]{:S(2)}) async-start(), calls=%async_computation.10 | async-start | bytes 4866048 | tf_op jit(solution)/shard_map/all_gather | solution.py:205
  10.0 335.6 %all-gather.14.cloned.1.call-start = ((), (), s32[]{:S(2)}) async-start(), calls=%async_computation.11 | async-start | bytes 4866048 | tf_op jit(solution)/shard_map/all_gather | solution.py:207
  59.7 106.8 %copy-start.59 = (f32[768]{0:T(1024)}, f32[768]{0:T(1024)S(1)}, u32[]{:S(2)}) copy-start(f32[768]{0:T(1024)S(1)} %convert_element_type.137) | copy-start | bytes 9220
  59.7 106.8 %copy-start.71 = (f32[768]{0:T(1024)}, f32[768]{0:T(1024)S(1)}, u32[]{:S(2)}) copy-start(f32[768]{0:T(1024)S(1)} %convert_element_type.138) | copy-start | bytes 9220
  101.1 65.0 %copy-start.11 = (f32[128,768]{1,0:T(8,128)}, f32[128,768]{1,0:T(8,128)S(1)}, u32[]{:S(2)}) copy-start(f32[128,768]{1,0:T(8,128)S(1)} %get-tuple-element.814) | copy-start | bytes 1179652
  101.1 59.7 %copy-start.3 = (bf16[2,128,6144]{2,1,0:T(8,128)(2,1)S(1)}, bf16[2,128,6144]{2,1,0:T(8,128)(2,1)}, u32[]{:S(2)}) copy-start(bf16[2,128,6144]{2,1,0:T(8,128)(2,1)} %param.33) | copy-start | bytes 9437188
  101.2 65.0 %copy-start.92 = (f32[128]{0:T(128)}, f32[128]{0:T(128)S(1)}, u32[]{:S(2)}) copy-start(f32[128]{0:T(128)S(1)} %broadcast_multiply_fusion.9) | copy-start | bytes 1540
  160.6 8.7 collective-permute-start.7
  166.2 40.3 %copy-start.121 = (bf16[768]{0:T(1024)(128)(2,1)S(1)}, bf16[768]{0:T(1024)(128)(2,1)}, u32[]{:S(2)}) copy-start(bf16[768]{0:T(1024)(128)(2,1)} %get-tuple-element.774) | copy-start | bytes 4612
  166.2 40.4 %copy-start.120 = (bf16[768]{0:T(1024)(128)(2,1)S(1)}, bf16[768]{0:T(1024)(128)(2,1)}, u32[]{:S(2)}) copy-start(bf16[768]{0:T(1024)(128)(2,1)} %get-tuple-element.773) | copy-start | bytes 4612
  166.2 40.4 %copy-start.119 = (bf16[768]{0:T(1024)(128)(2,1)S(1)}, bf16[768]{0:T(1024)(128)(2,1)}, u32[]{:S(2)}) copy-start(bf16[768]{0:T(1024)(128)(2,1)} %get-tuple-element.770) | copy-start | bytes 4612
  166.2 41.0 %copy-start.115 = (bf16[3072]{0:T(1024)(128)(2,1)S(1)}, bf16[3072]{0:T(1024)(128)(2,1)}, u32[]{:S(2)}) copy-start(bf16[3072]{0:T(1024)(128)(2,1)} %get-tuple-element.772) | copy-start | bytes 18436
  167.3 40.6 %slice-start.3 = ((bf16[128,2304]{1,0:T(8,128)(2,1)}), bf16[128,768]{1,0:T(8,128)(2,1)S(1)}, s32[]{:S(2)}) async-start(bf16[128,2304]{1,0:T(8,128)(2,1)} %copy-done.41), calls=%async_computation.22 | async-start | bytes 393216 | tf_op jit(solution)/shard_map/slice | solution.py:222
  168.1 58.9 %copy-start.42 = (bf16[128,2304]{1,0:T(8,128)(2,1)S(1)}, bf16[128,2304]{1,0:T(8,128)(2,1)}, u32[]{:S(2)}) copy-start(bf16[128,2304]{1,0:T(8,128)(2,1)} %copy-done.41) | copy-start | bytes 1769476
  168.1 10.3 collective-permute-start
  169.3 17.7 %collective-permute-start.8 = (bf16[128,1536]{1,0:T(8,128)(2,1)S(1)}, bf16[128,1536]{1,0:T(8,128)(2,1)S(1)}, u32[]{:S(2)}, u32[]{:S(2)}) collective-permute-start(bf16[128,1536]{1,0:T(8,128)(2,1)S(1)} %collective-permute-done.7), channel_id=1, source_target_pairs={{0,1},{1,2},{2,3},{3,4},{4,5},{5,6},{6,7},{7,0},{8,9},{9,10},{10,1... | collective-permute-start | bytes 1179656 | tf_op jit(solution)/shard_map/ppermute | solution.py:18
  169.7 17.3 %collective-permute-start.4 = (bf16[128,1536]{1,0:T(8,128)(2,1)S(1)}, bf16[128,1536]{1,0:T(8,128)(2,1)S(1)}, u32[]{:S(2)}, u32[]{:S(2)}) collective-permute-start(bf16[128,1536]{1,0:T(8,128)(2,1)S(1)} %slice.74), channel_id=1, source_target_pairs={{0,7},{1,0},{2,1},{3,2},{4,3},{5,4},{6,5},{7,6},{8,15},{9,8},{10,9... | collective-permute-start | bytes 1179656 | tf_op jit(solution)/shard_map/ppermute | solution.py:20
  171.9 19.1 %collective-permute-start.11 = (bf16[128,1536]{1,0:T(8,128)(2,1)S(1)}, bf16[128,1536]{1,0:T(8,128)(2,1)S(1)}, u32[]{:S(2)}, u32[]{:S(2)}) collective-permute-start(bf16[128,1536]{1,0:T(8,128)(2,1)S(1)} %slice.76), channel_id=1, source_target_pairs={{0,7},{1,0},{2,1},{3,2},{4,3},{5,4},{6,5},{7,6},{8,15},{9,8},{10,9... | collective-permute-start | bytes 1179656 | tf_op jit(solution)/shard_map/ppermute | solution.py:20
  178.4 18.0 %collective-permute-start.1 = (bf16[128,1536]{1,0:T(8,128)(2,1)S(1)}, bf16[128,1536]{1,0:T(8,128)(2,1)}, u32[]{:S(2)}, u32[]{:S(2)}) collective-permute-start(bf16[128,1536]{1,0:T(8,128)(2,1)S(1)} %collective-permute-done), channel_id=1, source_target_pairs={{0,1},{1,2},{2,3},{3,4},{4,5},{5,6},{6,7},{7,0},{8,9},{9,10},{10,1... | collective-permute-start | bytes 1179656 | tf_op jit(solution)/shard_map/ppermute | solution.py:18
  187.0 19.5 %collective-permute-start.9 = (bf16[128,1536]{1,0:T(8,128)(2,1)S(1)}, bf16[128,1536]{1,0:T(8,128)(2,1)}, u32[]{:S(2)}, u32[]{:S(2)}) collective-permute-start(bf16[128,1536]{1,0:T(8,128)(2,1)S(1)} %collective-permute-done.8), channel_id=1, source_target_pairs={{0,1},{1,2},{2,3},{3,4},{4,5},{5,6},{6,7},{7,0},{8,9},{9,10},{10,1... | collective-permute-start | bytes 1179656 | tf_op jit(solution)/shard_map/ppermute | solution.py:18
  187.0 21.2 %collective-permute-start.5 = (bf16[128,1536]{1,0:T(8,128)(2,1)S(1)}, bf16[128,1536]{1,0:T(8,128)(2,1)}, u32[]{:S(2)}, u32[]{:S(2)}) collective-permute-start(bf16[128,1536]{1,0:T(8,128)(2,1)S(1)} %collective-permute-done.4), channel_id=1, source_target_pairs={{0,7},{1,0},{2,1},{3,2},{4,3},{5,4},{6,5},{7,6},{8,15},{9,8},{10,9... | collective-permute-start | bytes 1179656 | tf_op jit(solution)/shard_map/ppermute | solution.py:20
  191.0 19.9 %collective-permute-start.12 = (bf16[128,1536]{1,0:T(8,128)(2,1)S(1)}, bf16[128,1536]{1,0:T(8,128)(2,1)}, u32[]{:S(2)}, u32[]{:S(2)}) collective-permute-start(bf16[128,1536]{1,0:T(8,128)(2,1)S(1)} %collective-permute-done.11), channel_id=1, source_target_pairs={{0,7},{1,0},{2,1},{3,2},{4,3},{5,4},{6,5},{7,6},{8,15},{9,8},{10,9... | collective-permute-start | bytes 1179656 | tf_op jit(solution)/shard_map/ppermute | solution.py:20
  196.4 19.0 %collective-permute-start.2 = (bf16[128,1536]{1,0:T(8,128)(2,1)}, bf16[128,1536]{1,0:T(8,128)(2,1)}, u32[]{:S(2)}, u32[]{:S(2)}) collective-permute-start(bf16[128,1536]{1,0:T(8,128)(2,1)} %collective-permute-done.1), channel_id=1, source_target_pairs={{0,1},{1,2},{2,3},{3,4},{4,5},{5,6},{6,7},{7,0},{8,9},{9,10},{10,1... | collective-permute-start | bytes 1179656 | tf_op jit(solution)/shard_map/ppermute | solution.py:18
  206.4 17.3 %collective-permute-start.10 = (bf16[128,1536]{1,0:T(8,128)(2,1)}, bf16[128,1536]{1,0:T(8,128)(2,1)}, u32[]{:S(2)}, u32[]{:S(2)}) collective-permute-start(bf16[128,1536]{1,0:T(8,128)(2,1)} %collective-permute-done.9), channel_id=1, source_target_pairs={{0,1},{1,2},{2,3},{3,4},{4,5},{5,6},{6,7},{7,0},{8,9},{9,10},{10,1... | collective-permute-start | bytes 1179656 | tf_op jit(solution)/shard_map/ppermute | solution.py:18
  206.5 246.7 %reduce-scatter.22.cloned.1.call-start = ((), (), s32[]{:S(2)}) async-start(), calls=%async_computation.16 | async-start | bytes 3538944
  208.2 27.2 %collective-permute-start.6 = (bf16[128,1536]{1,0:T(8,128)(2,1)}, bf16[128,1536]{1,0:T(8,128)(2,1)S(1)}, u32[]{:S(2)}, u32[]{:S(2)}) collective-permute-start(bf16[128,1536]{1,0:T(8,128)(2,1)} %collective-permute-done.5), channel_id=1, source_target_pairs={{0,7},{1,0},{2,1},{3,2},{4,3},{5,4},{6,5},{7,6},{8,15},{9,8},{10,9... | collective-permute-start | bytes 1179656 | tf_op jit(solution)/shard_map/ppermute | solution.py:20
  210.9 24.4 %collective-permute-start.13 = (bf16[128,1536]{1,0:T(8,128)(2,1)}, bf16[128,1536]{1,0:T(8,128)(2,1)S(1)}, u32[]{:S(2)}, u32[]{:S(2)}) collective-permute-start(bf16[128,1536]{1,0:T(8,128)(2,1)} %collective-permute-done.12), channel_id=1, source_target_pairs={{0,7},{1,0},{2,1},{3,2},{4,3},{5,4},{6,5},{7,6},{8,15},{9,8},{10,9... | collective-permute-start | bytes 1179656 | tf_op jit(solution)/shard_map/ppermute | solution.py:20
  215.3 15.7 %collective-permute-start.3 = (bf16[128,1536]{1,0:T(8,128)(2,1)}, bf16[128,1536]{1,0:T(8,128)(2,1)S(1)}, u32[]{:S(2)}, u32[]{:S(2)}) collective-permute-start(bf16[128,1536]{1,0:T(8,128)(2,1)} %collective-permute-done.2), channel_id=1, source_target_pairs={{0,1},{1,2},{2,3},{3,4},{4,5},{5,6},{6,7},{7,0},{8,9},{9,10},{10,1... | collective-permute-start | bytes 1179656 | tf_op jit(solution)/shard_map/ppermute | solution.py:18
  282.2 77.5 %copy-start.79 = (f32[128]{0:T(128)}, f32[128]{0:T(128)S(1)}, u32[]{:S(2)}) copy-start(f32[128]{0:T(128)S(1)} %broadcast_multiply_fusion.10) | copy-start | bytes 1540
  283.6 70.0 %copy-start.95 = (f32[128]{0:T(128)}, f32[128]{0:T(128)S(1)}, u32[]{:S(2)}) copy-start(f32[128]{0:T(128)S(1)} %add_rsqrt_fusion.2) | copy-start | bytes 1540
  392.8 110.3 %reduce-scatter.24.cloned.1.call-start = ((), (), s32[]{:S(2)}) async-start(), calls=%async_computation.17 | async-start | bytes 3538944
  407.9 217.2 %reduce-scatter.16.cloned.1.call-start = ((), (), s32[]{:S(2)}) async-start(), calls=%async_computation.13 | async-start | bytes 2433024 | tf_op jit(solution)/shard_map/reduce_scatter | solution.py:314
  411.4 338.9 %reduce-scatter.20.cloned.1.call-start = ((), (), s32[]{:S(2)}) async-start(), calls=%async_computation.15 | async-start | bytes 9732096 | tf_op jit(solution)/shard_map/reduce_scatter | solution.py:320
  419.0 471.9 %reduce-scatter.18.cloned.1.call-start = ((), (), s32[]{:S(2)}) async-start(), calls=%async_computation.14 | async-start | bytes 9732096 | tf_op jit(solution)/shard_map/reduce_scatter | solution.py:318
  426.9 77.5 %copy-start.60 = (f32[768]{0:T(1024)S(1)}, f32[768]{0:T(1024)}, u32[]{:S(2)}) copy-start(f32[768]{0:T(1024)} %copy-done.59) | copy-start | bytes 9220
  426.9 77.5 %copy-start.72 = (f32[768]{0:T(1024)S(1)}, f32[768]{0:T(1024)}, u32[]{:S(2)}) copy-start(f32[768]{0:T(1024)} %copy-done.71) | copy-start | bytes 9220
  426.9 77.5 %copy-start.99 = (f32[128]{0:T(128)S(1)}, f32[128]{0:T(128)}, u32[]{:S(2)}) copy-start(f32[128]{0:T(128)} %copy-done.98) | copy-start | bytes 1540
  426.9 77.5 %copy-start.113 = (f32[128]{0:T(128)S(1)}, f32[128]{0:T(128)}, u32[]{:S(2)}) copy-start(f32[128]{0:T(128)} %copy-done.112) | copy-start | bytes 1540
  426.9 77.5 %copy-start.17 = (f32[128,768]{1,0:T(8,128)S(1)}, f32[128,768]{1,0:T(8,128)}, u32[]{:S(2)}) copy-start(f32[128,768]{1,0:T(8,128)} %copy-done.16) | copy-start | bytes 1179652
  426.9 589.7 %reduce-scatter.14.cloned.1.call-start = ((), (), s32[]{:S(2)}) async-start(), calls=%async_computation.12 | async-start | bytes 7299072 | tf_op jit(solution)/shard_map/reduce_scatter | solution.py:313
  427.9 77.8 %copy-start.58 = (bf16[128,12,64]{0,2,1:T(8,128)(2,1)}, bf16[128,12,64]{0,2,1:T(8,128)(2,1)S(1)}, u32[]{:S(2)}) copy-start(bf16[128,12,64]{0,2,1:T(8,128)(2,1)S(1)} %multiply_convert_fusion.3) | copy-start | bytes 589828
  428.0 77.7 %copy-start.51 = (bf16[128,12,64]{0,2,1:T(8,128)(2,1)}, bf16[128,12,64]{0,2,1:T(8,128)(2,1)S(1)}, u32[]{:S(2)}) copy-start(bf16[128,12,64]{0,2,1:T(8,128)(2,1)S(1)} %multiply_convert_fusion.2) | copy-start | bytes 589828
  454.3 51.3 %copy-start.57 = (bf16[128,1536]{0,1:T(8,128)(2,1)}, bf16[128,1536]{0,1:T(8,128)(2,1)S(1)}, u32[]{:S(2)}) copy-start(bf16[128,1536]{0,1:T(8,128)(2,1)S(1)} %copy.106) | copy-start | bytes 1179652
  509.9 719.5 %reduce-scatter.26.cloned.1.call-start = ((), (), s32[]{:S(2)}) async-start(), calls=%async_computation.18 | async-start | bytes 19464192
  562.0 56.8 %slice-start = ((s8[9437184]{0:T(1024)(128)(4,1)}), s8[1048576]{0:T(1024)(128)(4,1)S(1)}, s32[]{:S(2)}) async-start(s8[9437184]{0:T(1024)(128)(4,1)} %bitcast.411), calls=%async_computation.19 | async-start | bytes 2097152
  (106 other events, 299.0 us)
Sparse Core Ops, SparseCore 0:
  10.9 84.5 all-gather.5
  98.4 58.6 all-gather.7
  160.0 54.9 all-gather.9
  217.7 62.6 all-gather.11
  283.1 62.4 all-gather.13
  392.9 60.1 reduce-scatter.21
  456.9 46.2 reduce-scatter.23
  509.0 99.2 reduce-scatter.15
  615.8 134.4 reduce-scatter.19
  756.6 134.3 reduce-scatter.17
  898.2 118.3 reduce-scatter.13
  1023.4 206.0 reduce-scatter.25
